TPU v7x, 1024 devices: a whole 4x8x16 slice. The times are simulated.
1024 devices in a mesh: pipe: 16 (over z), expert: 16 (over x, y_hi), tensor: 4 (over y_lo, core).
Axes of the slice: x: 4, y: 8 (y_hi: 4, y_lo: 2; y = y_hi * 2 + y_lo), z: 16, core: 2. Of those that a mesh axis runs over, the one named last changes fastest.
Arguments:
- acts: bfloat16 [16, 16, 256, 1792], P('pipe', 'expert'), may hold values from -6 to 6
- hidden_grad: bfloat16 [16, 8, 256, 1024], P('pipe', None, None, 'tensor'), may hold values from -0.5 to 0.5
- counts: int32 [16, 8, 2], P('pipe'), may hold values from 32 to 128, as said below
- momentum: bfloat16 [16, 16, 1792, 1024], P('pipe', 'expert', 'tensor'), may hold values from -6 to 6
- act_grad: bfloat16 [16, 1024, 7168], P('pipe', 'expert', 'tensor'), may hold values from -6 to 6
Outputs:
- new_momentum: bfloat16 [16, 16, 1792, 1024], P('pipe', 'expert', 'tensor')
- gram_rows: float32 [16, 16, 256, 1024], P('pipe', 'expert', 'tensor')
- received: bfloat16 [16, 1024, 7168], P('pipe', 'expert', 'tensor')
Inputs may be any that keep to these rules, and one draw needn't show every extreme that they name: `counts`: in every section and expert, at least one micro-batch fills its block.
All inputs are finite; a program needn't handle non-finite values.
Results may differ from a plain program's by a relative error of at most 0.0065.
Values may be sent and summed in bfloat16 or wider, within the bound.
No kernel may reach another device: no remote copies, remote signals or barrier semaphores. Data moves between devices by JAX's collectives and lax.ppermute only.
A program may use at most 32 MiB of HBM per device.

v0:
```python
import jax
import jax.numpy as jnp
from jax import lax
from jax.experimental import pallas as pl
from jax.experimental.pallas import tpu as pltpu
from jax.sharding import PartitionSpec as P


D = 3584
PANEL = 512
Y_HI = 4
DECAY = 0.9


def fetch(grad_ref, acts_ref, mine_ref, other_ref, window_ref, sems):
    t, e = lax.axis_index("tensor"), lax.axis_index("expert")
    width = window_ref.shape[1]
    start = pl.multiple_of(t // 2 * width, 128)
    copies = [
        pltpu.make_async_copy(grad_ref.at[0, e // 2], mine_ref, sems.at[0]),
        pltpu.make_async_copy(grad_ref.at[0, neighbour(e, t) // 2], other_ref, sems.at[1]),
        pltpu.make_async_copy(acts_ref.at[0, 0, :, pl.ds(start, width)], window_ref, sems.at[2]),
    ]
    for copy in copies:
        copy.start()
    for copy in copies:
        copy.wait()


def prepare(window_ref, counts_ref, xt_ref):
    pair = lax.axis_index("expert") // 2
    rows, width = window_ref.shape
    micro = counts_ref.shape[2]
    block = rows // micro
    row = lax.broadcasted_iota(jnp.int32, (block, width), 0)
    for m in range(micro):
        part = window_ref[m * block : (m + 1) * block, :]
        part = jnp.where(row < counts_ref[0, pair, m], part, jnp.zeros_like(part))
        xt_ref[:, m * block : (m + 1) * block] = part.T


def main(xt_ref, h0, h1, h2, h3, own_ref, mate_ref, new_ref, keep_ref, near_ref, side_ref, far_ref, full, gram, sem):
    t = lax.axis_index("tensor")
    half = lax.axis_index("expert") % 2
    core, chip = t % 2, t // 2
    rows = own_ref.shape[0]
    for k, piece in enumerate((h0, h1, h2, h3)):
        width = piece.shape[1]
        col = pl.multiple_of(jnp.bitwise_xor(t, k) * width, 128)
        for i, (who, moment) in enumerate(((core, own_ref), (1 - core, mate_ref))):
            x = xt_ref[pl.ds(pl.multiple_of(who * rows, 64), rows), :]
            grad = jnp.dot(x, piece[...], preferred_element_type=jnp.float32).astype(jnp.bfloat16)
            new = DECAY * moment[:, pl.ds(col, width)].astype(jnp.float32) + grad.astype(jnp.float32)
            new = new.astype(jnp.bfloat16)
            full[i * rows : (i + 1) * rows, pl.ds(col, width)] = new
    store = pltpu.make_async_copy(full.at[pl.ds(0, rows)], new_ref, sem)
    store.start()
    share = gram.shape[0] // 2
    for i in range(2):
        left = full[:, pl.ds(pl.multiple_of((2 * i + core) * share, 128), share)]
        gram[i * share : (i + 1) * share, :] = jnp.dot(left.T, full[...], preferred_element_type=jnp.float32)
    quarter = share // 2

    def block(which, side):
        return gram[pl.ds(pl.multiple_of(which * share + side * quarter, 64), quarter), :]

    near_ref[...] = block(1 - chip, half).astype(jnp.bfloat16)
    side_ref[...] = block(chip, 1 - half).astype(jnp.bfloat16)
    far_ref[...] = block(1 - chip, 1 - half).astype(jnp.bfloat16)
    keep_ref[...] = block(chip, half)
    store.wait()


def finish(keep_ref, near_ref, side_ref, far_ref, arrived_ref, gram_ref, received_ref, sem):
    store = pltpu.make_async_copy(arrived_ref, received_ref, sem)
    store.start()
    total = keep_ref[...] + near_ref[...].astype(jnp.float32)
    total += side_ref[...].astype(jnp.float32) + far_ref[...].astype(jnp.float32)
    gram_ref[...] = total / D
    store.wait()


def neighbour(e, t):
    return e // Y_HI * Y_HI + lax.rem(e % Y_HI + jnp.where(t >= 2, 1, Y_HI - 1), Y_HI)


def flip(array, expert_bit, tensor_bits):
    ne, nt = lax.axis_size("expert"), lax.axis_size("tensor")
    route = [
        (e * nt + t, (e ^ expert_bit) * nt + (t ^ tensor_bits)) for e in range(ne) for t in range(nt)
    ]
    return lax.ppermute(array, ("expert", "tensor"), route)


def across(array):
    ne, nt = lax.axis_size("expert"), lax.axis_size("tensor")
    route = []
    for e in range(ne):
        for t in range(nt):
            y_hi = (e % Y_HI + (1 if t // 2 else -1)) % Y_HI
            route.append((e * nt + t, (e // Y_HI * Y_HI + y_hi) * nt + (t ^ 3)))
    return lax.ppermute(array, ("expert", "tensor"), route)


def on_device(acts, hidden_grad, counts, momentum, act_grad):
    n_tensor = lax.axis_size("tensor")
    sections = lax.axis_size("pipe")
    _, _, rows, _ = acts.shape
    own_rows, hidden = momentum.shape[2:]
    slice_width = hidden_grad.shape[3]
    quarter = PANEL // (2 * n_tensor)
    bf16, f32 = jnp.bfloat16, jnp.float32
    vmem = pl.BlockSpec(memory_space=pltpu.VMEM)
    hbm = pl.BlockSpec(memory_space=pltpu.HBM)
    shape = jax.ShapeDtypeStruct

    mine, other, window = pl.pallas_call(
        fetch,
        out_shape=(shape((rows, slice_width), bf16),) * 2 + (shape((rows, 2 * own_rows), bf16),),
        in_specs=[hbm, hbm],
        out_specs=(vmem,) * 3,
        scratch_shapes=[pltpu.SemaphoreType.DMA((3,))],
        compiler_params=pltpu.CompilerParams(vmem_limit_bytes=8 << 20),
        cost_estimate=pl.CostEstimate(flops=0, bytes_accessed=4 * rows * own_rows * 2, transcendentals=0),
        name="fetch",
    )(pltpu.with_memory_space_constraint(hidden_grad, pltpu.HBM), pltpu.with_memory_space_constraint(acts, pltpu.HBM))
    h2 = flip(mine, 0, 2)
    h3 = across(other)
    own = momentum[0, 0]
    mate = flip(own, 0, 1)
    h1 = flip(mine, 0, 1)
    xt = pl.pallas_call(
        prepare,
        out_shape=shape((2 * own_rows, rows), bf16),
        in_specs=[vmem, pl.BlockSpec(memory_space=pltpu.SMEM)],
        out_specs=vmem,
        compiler_params=pltpu.CompilerParams(vmem_limit_bytes=8 << 20),
        cost_estimate=pl.CostEstimate(flops=0, bytes_accessed=4 * rows * own_rows * 2, transcendentals=0),
        name="prepare",
    )(window, counts)
    block = shape((quarter, hidden), bf16)
    new, keep, near, side, far = pl.pallas_call(
        main,
        out_shape=(shape((own_rows, hidden), bf16), shape((quarter, hidden), f32), block, block, block),
        in_specs=[vmem] * 7,
        out_specs=(hbm,) + (vmem,) * 4,
        scratch_shapes=[
            pltpu.VMEM((2 * own_rows, hidden), bf16),
            pltpu.VMEM((PANEL // 2, hidden), f32),
            pltpu.SemaphoreType.DMA,
        ],
        compiler_params=pltpu.CompilerParams(vmem_limit_bytes=20 << 20),
        cost_estimate=pl.CostEstimate(
            flops=4 * own_rows * hidden * (rows + PANEL // 2),
            bytes_accessed=8 * own_rows * hidden,
            transcendentals=0,
        ),
        name="gradients",
    )(xt, mine, h1, h2, h3, own, mate)
    far = flip(far, 1, 2)
    arrived = lax.ppermute(act_grad[0], "pipe", [(i + 1, i) for i in range(sections - 1)])
    side = flip(side, 1, 0)
    near = flip(near, 0, 2)
    gram, received = pl.pallas_call(
        finish,
        out_shape=(shape((quarter, hidden), f32), shape(arrived.shape, bf16)),
        in_specs=[vmem] * 4 + [pl.BlockSpec(memory_space=pl.ANY)],
        out_specs=(vmem, hbm),
        scratch_shapes=[pltpu.SemaphoreType.DMA],
        compiler_params=pltpu.CompilerParams(vmem_limit_bytes=8 << 20),
        cost_estimate=pl.CostEstimate(flops=0, bytes_accessed=20 * quarter * hidden, transcendentals=0),
        name="finish",
    )(keep, near, side, far, arrived)
    return new[None, None], gram[None, None], received[None]


def solution(mesh):
    return jax.shard_map(
        on_device,
        mesh=mesh,
        in_specs=(
            P("pipe", "expert", None, None),
            P("pipe", None, None, "tensor"),
            P("pipe", None, None),
            P("pipe", "expert", "tensor", None),
            P("pipe", "expert", "tensor"),
        ),
        out_specs=(
            P("pipe", "expert", "tensor", None),
            P("pipe", "expert", "tensor", None),
            P("pipe", "expert", "tensor"),
        ),
        check_vma=False,
    )
```

profile of v0, /device:TPU:8, one launch (start us, length us, event | category | flops | bytes accessed | tf_op | source)
XLA Modules:
  0.0 51.1 jit_solution(5247338245657427010)
XLA Ops:
  0.6 0.0 copy-start.2
  0.6 2.1 %collective-permute-start.3 = (bf16[448,1024]{1,0:T(8,128)(2,1)}, bf16[448,1024]{1,0:T(8,128)(2,1)S(1)}, u32[]{:S(2)}, u32[]{:S(2)}) collective-permute-start(bf16[448,1024]{1,0:T(8,128)(2,1)} %bitcast.5), channel_id=1, source_target_pairs={{0,1},{1,0},{2,3},{3,2},{4,5},{5,4},{6,7},{7,6},{8,9},{9,8},{10,11... | collective-permute-start | bytes 2752520 | tf_op jit(solution)/shard_map/ppermute | solution.py:92
  2.7 0.0 copy-start.1
  2.7 1.2 %fetch.1 = (bf16[256,256]{1,0:T(8,128)(2,1)S(1)}, bf16[256,256]{1,0:T(8,128)(2,1)S(1)}, bf16[256,896]{1,0:T(8,128)(2,1)S(1)}) custom-call(bf16[1,8,256,256]{3,2,1,0:T(8,128)(2,1)} %grad_ref.1, bf16[1,1,256,1792]{3,2,1,0:T(8,128)(2,1)} %acts_ref.1), custom_call_target="tpu_custom_call" | custom-call | bytes 917504 | tf_op jit(solution)/shard_map/fetch/pallas_call | solution.py:117
  3.9 0.0 copy-start
  3.9 2.5 %collective-permute-start = (bf16[256,256]{1,0:T(8,128)(2,1)S(1)}, bf16[256,256]{1,0:T(8,128)(2,1)S(1)}, u32[]{:S(2)}, u32[]{:S(2)}) collective-permute-start(bf16[256,256]{1,0:T(8,128)(2,1)S(1)} %get-tuple-element.14.h0), channel_id=1, source_target_pairs={{0,1},{1,0},{2,3},{3,2},{4,5},{5,4},{6,7},{7,6},{8,9},{9,8},{10,11... | collective-permute-start | bytes 393224 | tf_op jit(solution)/shard_map/ppermute | solution.py:92
  6.5 15.0 %collective-permute-start.1 = (bf16[256,256]{1,0:T(8,128)(2,1)S(1)}, bf16[256,256]{1,0:T(8,128)(2,1)S(1)}, u32[]{:S(2)}, u32[]{:S(2)}) collective-permute-start(bf16[256,256]{1,0:T(8,128)(2,1)S(1)} %get-tuple-element.14.h0), channel_id=1, source_target_pairs={{0,2},{1,3},{2,0},{3,1},{4,6},{5,7},{6,4},{7,5},{8,10},{9,11},{10,... | collective-permute-start | bytes 393224 | tf_op jit(solution)/shard_map/ppermute | solution.py:92
  21.5 1.9 %collective-permute-start.2 = (bf16[256,256]{1,0:T(8,128)(2,1)S(1)}, bf16[256,256]{1,0:T(8,128)(2,1)S(1)}, u32[]{:S(2)}, u32[]{:S(2)}) collective-permute-start(bf16[256,256]{1,0:T(8,128)(2,1)S(1)} %get-tuple-element.15), channel_id=1, source_target_pairs={{0,15},{1,14},{2,5},{3,4},{4,3},{5,2},{6,9},{7,8},{8,7},{9,6},{10,... | collective-permute-start | bytes 393224 | tf_op jit(solution)/shard_map/ppermute | solution.py:102
  23.4 0.0 copy-done.2
  23.4 1.3 %collective-permute-start.7 = (bf16[64,1792]{1,0:T(8,128)(2,1)S(1)}, bf16[64,1792]{1,0:T(8,128)(2,1)S(1)}, u32[]{:S(2)}, u32[]{:S(2)}) collective-permute-start(bf16[64,1792]{1,0:T(8,128)(2,1)S(1)} %bitcast.8), channel_id=1, source_target_pairs={{64,0},{128,64},{192,128},{256,192},{320,256},{384,320},{448,384},... | collective-permute-start | bytes 688136 | tf_op jit(solution)/shard_map/ppermute | solution.py:161
  24.7 0.0 copy-done.1
  24.7 0.1 copy.8.counts_ref
  24.8 0.8 %prepare.1.xt_ref = bf16[896,256]{1,0:T(8,128)(2,1)S(1)} custom-call(bf16[256,896]{1,0:T(8,128)(2,1)S(1)} %get-tuple-element.13.window_ref, s32[1,8,2]{2,1,0:T(8,128)S(1)} %copy.8.counts_ref), custom_call_target="tpu_custom_call" | custom-call | bytes 917504 | tf_op jit(solution)/shard_map/prepare/pallas_call | solution.py:132
  25.6 0.0 collective-permute-done.h1
  25.6 0.0 collective-permute-done.1.h2
  25.6 3.5 %collective-permute-done.2.h3 = bf16[256,256]{1,0:T(8,128)(2,1)S(1)} collective-permute-done((bf16[256,256]{1,0:T(8,128)(2,1)S(1)}, bf16[256,256]{1,0:T(8,128)(2,1)S(1)}, u32[]{:S(2)}, u32[]{:S(2)}) %collective-permute-start.2) | collective-permute-done | bytes 131104 | tf_op jit(solution)/shard_map/ppermute | solution.py:102
  29.1 0.0 collective-permute-done.3.mate_ref
  29.1 0.0 copy-done
  29.1 1.8 %gradients.1 = (bf16[448,1024]{1,0:T(8,128)(2,1)}, f32[64,1024]{1,0:T(8,128)S(1)}, bf16[64,1024]{1,0:T(8,128)(2,1)S(1)}, bf16[64,1024]{1,0:T(8,128)(2,1)S(1)}, bf16[64,1024]{1,0:T(8,128)(2,1)S(1)}) custom-call(bf16[896,256]{1,0:T(8,128)(2,1)S(1)} %prepare.1.xt_ref, bf16[256,256]{1,0:T(8,128)(2,1)S(1)} %get-tuple-element.14.h0, ...), custom_call_target="tpu_custom_call" | custom-call | flops 939524096 | bytes 3670016 | tf_op jit(solution)/shard_map/gradients/pallas_call | solution.py:142
  30.8 3.0 %collective-permute-start.4 = (bf16[64,1024]{1,0:T(8,128)(2,1)S(1)}, bf16[64,1024]{1,0:T(8,128)(2,1)S(1)}, u32[]{:S(2)}, u32[]{:S(2)}) collective-permute-start(bf16[64,1024]{1,0:T(8,128)(2,1)S(1)} %get-tuple-element.18), channel_id=1, source_target_pairs={{0,2},{1,3},{2,0},{3,1},{4,6},{5,7},{6,4},{7,5},{8,10},{9,11},{10,... | collective-permute-start | bytes 393224 | tf_op jit(solution)/shard_map/ppermute | solution.py:92
  33.9 1.9 %collective-permute-start.5 = (bf16[64,1024]{1,0:T(8,128)(2,1)S(1)}, bf16[64,1024]{1,0:T(8,128)(2,1)S(1)}, u32[]{:S(2)}, u32[]{:S(2)}) collective-permute-start(bf16[64,1024]{1,0:T(8,128)(2,1)S(1)} %get-tuple-element.19), channel_id=1, source_target_pairs={{0,4},{1,5},{2,6},{3,7},{4,0},{5,1},{6,2},{7,3},{8,12},{9,13},{10,... | collective-permute-start | bytes 393224 | tf_op jit(solution)/shard_map/ppermute | solution.py:92
  35.8 4.3 %collective-permute-start.6 = (bf16[64,1024]{1,0:T(8,128)(2,1)S(1)}, bf16[64,1024]{1,0:T(8,128)(2,1)S(1)}, u32[]{:S(2)}, u32[]{:S(2)}) collective-permute-start(bf16[64,1024]{1,0:T(8,128)(2,1)S(1)} %get-tuple-element.20), channel_id=1, source_target_pairs={{0,6},{1,7},{2,4},{3,5},{4,2},{5,3},{6,0},{7,1},{8,14},{9,15},{10,... | collective-permute-start | bytes 393224 | tf_op jit(solution)/shard_map/ppermute | solution.py:92
  40.1 0.0 collective-permute-done.7.arrived_ref
  40.1 0.0 collective-permute-done.4.near_ref
  40.1 4.9 %collective-permute-done.5.side_ref = bf16[64,1024]{1,0:T(8,128)(2,1)S(1)} collective-permute-done((bf16[64,1024]{1,0:T(8,128)(2,1)S(1)}, bf16[64,1024]{1,0:T(8,128)(2,1)S(1)}, u32[]{:S(2)}, u32[]{:S(2)}) %collective-permute-start.5) | collective-permute-done | bytes 131104 | tf_op jit(solution)/shard_map/ppermute | solution.py:92
  45.0 4.7 %collective-permute-done.6.far_ref = bf16[64,1024]{1,0:T(8,128)(2,1)S(1)} collective-permute-done((bf16[64,1024]{1,0:T(8,128)(2,1)S(1)}, bf16[64,1024]{1,0:T(8,128)(2,1)S(1)}, u32[]{:S(2)}, u32[]{:S(2)}) %collective-permute-start.6) | collective-permute-done | bytes 131104 | tf_op jit(solution)/shard_map/ppermute | solution.py:92
  49.7 1.4 %finish.1 = (f32[64,1024]{1,0:T(8,128)}, bf16[64,1792]{1,0:T(8,128)(2,1)}) custom-call(f32[64,1024]{1,0:T(8,128)S(1)} %get-tuple-element.17.keep_ref, bf16[64,1024]{1,0:T(8,128)(2,1)S(1)} %collective-permute-done.4.near_ref, bf16[64,1024]{1,0:T(8,128)(2,1)S(1)} %collective-permute-done.5.side_ref, bf16[64,1024]{1,0:T(8,128)(2,1)S(1)} %collective-permute-done.6.far_ref, ...), custom_call_target="tpu_custom_call" | custom-call | bytes 1310720 | tf_op jit(solution)/shard_map/finish/pallas_call | solution.py:164
Async XLA Ops:
  0.6 22.8 %copy-start.2 = (bf16[1,64,1792]{2,1,0:T(8,128)(2,1)S(1)}, bf16[1,64,1792]{2,1,0:T(8,128)(2,1)}, u32[]{:S(2)}) copy-start(bf16[1,64,1792]{2,1,0:T(8,128)(2,1)} %param.9) | copy-start | bytes 688132
  0.6 28.4 %collective-permute-start.3 = (bf16[448,1024]{1,0:T(8,128)(2,1)}, bf16[448,1024]{1,0:T(8,128)(2,1)S(1)}, u32[]{:S(2)}, u32[]{:S(2)}) collective-permute-start(bf16[448,1024]{1,0:T(8,128)(2,1)} %bitcast.5), channel_id=1, source_target_pairs={{0,1},{1,0},{2,3},{3,2},{4,5},{5,4},{6,7},{7,6},{8,9},{9,8},{10,11... | collective-permute-start | bytes 2752520 | tf_op jit(solution)/shard_map/ppermute | solution.py:92
  2.7 22.0 %copy-start.1 = (s32[1,8,2]{1,2,0:T(2,128)S(1)}, s32[1,8,2]{1,2,0:T(2,128)}, u32[]{:S(2)}) copy-start(s32[1,8,2]{1,2,0:T(2,128)} %param.7) | copy-start | bytes 196
  3.9 25.2 %copy-start = (bf16[1,1,448,1024]{3,2,1,0:T(8,128)(2,1)S(1)}, bf16[1,1,448,1024]{3,2,1,0:T(8,128)(2,1)}, u32[]{:S(2)}) copy-start(bf16[1,1,448,1024]{3,2,1,0:T(8,128)(2,1)} %param.8) | copy-start | bytes 2752516
  3.9 21.7 %collective-permute-start = (bf16[256,256]{1,0:T(8,128)(2,1)S(1)}, bf16[256,256]{1,0:T(8,128)(2,1)S(1)}, u32[]{:S(2)}, u32[]{:S(2)}) collective-permute-start(bf16[256,256]{1,0:T(8,128)(2,1)S(1)} %get-tuple-element.14.h0), channel_id=1, source_target_pairs={{0,1},{1,0},{2,3},{3,2},{4,5},{5,4},{6,7},{7,6},{8,9},{9,8},{10,11... | collective-permute-start | bytes 393224 | tf_op jit(solution)/shard_map/ppermute | solution.py:92
  6.5 19.1 %collective-permute-start.1 = (bf16[256,256]{1,0:T(8,128)(2,1)S(1)}, bf16[256,256]{1,0:T(8,128)(2,1)S(1)}, u32[]{:S(2)}, u32[]{:S(2)}) collective-permute-start(bf16[256,256]{1,0:T(8,128)(2,1)S(1)} %get-tuple-element.14.h0), channel_id=1, source_target_pairs={{0,2},{1,3},{2,0},{3,1},{4,6},{5,7},{6,4},{7,5},{8,10},{9,11},{10,... | collective-permute-start | bytes 393224 | tf_op jit(solution)/shard_map/ppermute | solution.py:92
  21.5 7.6 %collective-permute-start.2 = (bf16[256,256]{1,0:T(8,128)(2,1)S(1)}, bf16[256,256]{1,0:T(8,128)(2,1)S(1)}, u32[]{:S(2)}, u32[]{:S(2)}) collective-permute-start(bf16[256,256]{1,0:T(8,128)(2,1)S(1)} %get-tuple-element.15), channel_id=1, source_target_pairs={{0,15},{1,14},{2,5},{3,4},{4,3},{5,2},{6,9},{7,8},{8,7},{9,6},{10,... | collective-permute-start | bytes 393224 | tf_op jit(solution)/shard_map/ppermute | solution.py:102
  23.4 16.7 %collective-permute-start.7 = (bf16[64,1792]{1,0:T(8,128)(2,1)S(1)}, bf16[64,1792]{1,0:T(8,128)(2,1)S(1)}, u32[]{:S(2)}, u32[]{:S(2)}) collective-permute-start(bf16[64,1792]{1,0:T(8,128)(2,1)S(1)} %bitcast.8), channel_id=1, source_target_pairs={{64,0},{128,64},{192,128},{256,192},{320,256},{384,320},{448,384},... | collective-permute-start | bytes 688136 | tf_op jit(solution)/shard_map/ppermute | solution.py:161
  30.8 9.3 %collective-permute-start.4 = (bf16[64,1024]{1,0:T(8,128)(2,1)S(1)}, bf16[64,1024]{1,0:T(8,128)(2,1)S(1)}, u32[]{:S(2)}, u32[]{:S(2)}) collective-permute-start(bf16[64,1024]{1,0:T(8,128)(2,1)S(1)} %get-tuple-element.18), channel_id=1, source_target_pairs={{0,2},{1,3},{2,0},{3,1},{4,6},{5,7},{6,4},{7,5},{8,10},{9,11},{10,... | collective-permute-start | bytes 393224 | tf_op jit(solution)/shard_map/ppermute | solution.py:92
  33.9 11.1 %collective-permute-start.5 = (bf16[64,1024]{1,0:T(8,128)(2,1)S(1)}, bf16[64,1024]{1,0:T(8,128)(2,1)S(1)}, u32[]{:S(2)}, u32[]{:S(2)}) collective-permute-start(bf16[64,1024]{1,0:T(8,128)(2,1)S(1)} %get-tuple-element.19), channel_id=1, source_target_pairs={{0,4},{1,5},{2,6},{3,7},{4,0},{5,1},{6,2},{7,3},{8,12},{9,13},{10,... | collective-permute-start | bytes 393224 | tf_op jit(solution)/shard_map/ppermute | solution.py:92
  35.8 13.9 %collective-permute-start.6 = (bf16[64,1024]{1,0:T(8,128)(2,1)S(1)}, bf16[64,1024]{1,0:T(8,128)(2,1)S(1)}, u32[]{:S(2)}, u32[]{:S(2)}) collective-permute-start(bf16[64,1024]{1,0:T(8,128)(2,1)S(1)} %get-tuple-element.20), channel_id=1, source_target_pairs={{0,6},{1,7},{2,4},{3,5},{4,2},{5,3},{6,0},{7,1},{8,14},{9,15},{10,... | collective-permute-start | bytes 393224 | tf_op jit(solution)/shard_map/ppermute | solution.py:92
where the time goes:
time: 51.4 us; the launch traced here: 51.1 us
  starting transfers between devices  32 us (62%)
  waiting for transfers between devices  13 us (25%)
  Pallas kernels  5.15 us (10%)
  between operations  0.79 us (2%)
    ppermute x6, starting transfers between devices, flip(): return lax.ppermute(array, ('expert', 'tensor'), route)  28.8 us
    ppermute x6, waiting for transfers between devices, flip(): return lax.ppermute(array, ('expert', 'tensor'), route)  9.59 us
    ppermute x1, waiting for transfers between devices, across(): return lax.ppermute(array, ('expert', 'tensor'), route)  3.45 us
    ppermute x1, starting transfers between devices, across(): return lax.ppermute(array, ('expert', 'tensor'), route)  1.92 us
    pallas_call x1, Pallas kernels, on_device(): pl.pallas_call(main, out_shape=(shape((own_rows, hidden), bf16), shape((q...  1.76 us
    pallas_call x1, Pallas kernels, on_device(): pl.pallas_call(finish, out_shape=(shape((quarter, hidden), f32), shape(ar...  1.4 us
    ppermute x1, starting transfers between devices, on_device(): lax.ppermute(act_grad[0], 'pipe', [(i + 1, i) for i in range(sections - 1)])  1.29 us
    pallas_call x1, Pallas kernels, on_device(): pl.pallas_call(fetch, out_shape=(shape((rows, slice_width), bf16),) * 2 +...  1.2 us
  transfers between devices with their start and end apart: 8, of which 3 were waited for; matrix products, arithmetic and copies ran while one was open for 0% of the time, Pallas kernels for 7%

commit v1 on v0

v1 whole, which is shorter than its diff:
```python
import jax
import jax.numpy as jnp
from jax import lax
from jax.experimental import pallas as pl
from jax.experimental.pallas import tpu as pltpu
from jax.sharding import PartitionSpec as P


D = 3584
PANEL = 512
Y_HI = 4
DECAY = 0.9


def run_copies(moves, sems):
    copies = [pltpu.make_async_copy(source, target, sems.at[i]) for i, (source, target) in enumerate(moves)]
    for copy in copies:
        copy.start()
    for copy in copies:
        copy.wait()


def fetch(grad_ref, outer_ref, cross_ref, sems):
    t, e = lax.axis_index("tensor"), lax.axis_index("expert")
    run_copies(
        [(grad_ref.at[0, along(e, t) // 2], outer_ref), (grad_ref.at[0, diagonal(e, t) // 2], cross_ref)], sems
    )


def pack(grad_ref, acts_ref, moment_ref, packed_ref, window_ref, sems):
    t, e = lax.axis_index("tensor"), lax.axis_index("expert")
    width = window_ref.shape[1]
    start = pl.multiple_of(t // 2 * width, 128)
    rows = moment_ref.shape[2]
    deep, wide = packed_ref.shape[0] - rows, grad_ref.shape[3]
    moves = [(moment_ref.at[0, 0], packed_ref.at[pl.ds(0, rows)])]
    for k in range(packed_ref.shape[1] // wide):
        moves.append(
            (grad_ref.at[0, e // 2, pl.ds(k * deep, deep)], packed_ref.at[pl.ds(rows, deep), pl.ds(k * wide, wide)])
        )
    moves.append((acts_ref.at[0, 0, :, pl.ds(start, width)], window_ref))
    run_copies(moves, sems)


def prepare(window_ref, counts_ref, xt_ref):
    pair = lax.axis_index("expert") // 2
    rows, width = window_ref.shape
    micro = counts_ref.shape[2]
    block = rows // micro
    row = lax.broadcasted_iota(jnp.int32, (block, width), 0)
    for m in range(micro):
        part = window_ref[m * block : (m + 1) * block, :]
        part = jnp.where(row < counts_ref[0, pair, m], part, jnp.zeros_like(part))
        xt_ref[:, m * block : (m + 1) * block] = part.T


def main(xt_ref, own_ref, h2, h3, mate_ref, new_ref, keep_ref, near_ref, side_ref, far_ref, full, gram, sem):
    t = lax.axis_index("tensor")
    half = lax.axis_index("expert") % 2
    core, chip = t % 2, t // 2
    rows = new_ref.shape[0]
    width = h2.shape[1]
    deep = own_ref.shape[0] - rows
    unpack = lambda ref: jnp.concatenate([ref[rows:, k * width : (k + 1) * width] for k in range(h2.shape[0] // deep)])
    for k, piece in enumerate((unpack(own_ref), unpack(mate_ref), h2[...], h3[...])):
        col = pl.multiple_of(jnp.bitwise_xor(t, k) * width, 128)
        for i, (who, moment) in enumerate(((core, own_ref), (1 - core, mate_ref))):
            x = xt_ref[pl.ds(pl.multiple_of(who * rows, 64), rows), :]
            grad = jnp.dot(x, piece, preferred_element_type=jnp.float32).astype(jnp.bfloat16)
            new = DECAY * moment[:rows, pl.ds(col, width)].astype(jnp.float32) + grad.astype(jnp.float32)
            full[i * rows : (i + 1) * rows, pl.ds(col, width)] = new.astype(jnp.bfloat16)
    store = pltpu.make_async_copy(full.at[pl.ds(0, rows)], new_ref, sem)
    store.start()
    share = gram.shape[0] // 2
    left = [full[:, pl.ds(pl.multiple_of((2 * i + core) * share, 128), share)].T for i in range(2)]
    gram[...] = jnp.dot(jnp.concatenate(left), full[...], preferred_element_type=jnp.float32)
    quarter = share // 2

    def block(which, side):
        return gram[pl.ds(pl.multiple_of(which * share + side * quarter, 64), quarter), :]

    near_ref[...] = block(1 - chip, half).astype(jnp.bfloat16)
    side_ref[...] = block(chip, 1 - half).astype(jnp.bfloat16)
    far_ref[...] = block(1 - chip, 1 - half).astype(jnp.bfloat16)
    keep_ref[...] = block(chip, half)
    store.wait()


def finish(keep_ref, near_ref, side_ref, far_ref, arrived_ref, gram_ref, received_ref, total_ref, sems):
    relay = pltpu.make_async_copy(arrived_ref, received_ref, sems.at[0])
    relay.start()
    total = keep_ref[...] + near_ref[...].astype(jnp.float32)
    total += side_ref[...].astype(jnp.float32) + far_ref[...].astype(jnp.float32)
    total_ref[...] = total / D
    store = pltpu.make_async_copy(total_ref, gram_ref, sems.at[1])
    store.start()
    relay.wait()
    store.wait()


def along(e, t):
    return e // Y_HI * Y_HI + (e % Y_HI + (t // 2 * 2 - 1) + Y_HI) % Y_HI


def diagonal(e, t):
    count = lax.axis_size("expert")
    return (e + (t // 2 * 2 - 1) * Y_HI + count) % count


def flip(array, expert_bit, tensor_bits):
    ne, nt = lax.axis_size("expert"), lax.axis_size("tensor")
    route = [
        (e * nt + t, (e ^ expert_bit) * nt + (t ^ tensor_bits)) for e in range(ne) for t in range(nt)
    ]
    return lax.ppermute(array, ("expert", "tensor"), route)


def exchange(array, partner, flipped):
    ne, nt = lax.axis_size("expert"), lax.axis_size("tensor")
    route = [(e * nt + t, partner(e, t) * nt + (t ^ flipped)) for e in range(ne) for t in range(nt)]
    return lax.ppermute(array, ("expert", "tensor"), route)


def on_device(acts, hidden_grad, counts, momentum, act_grad):
    n_tensor = lax.axis_size("tensor")
    sections = lax.axis_size("pipe")
    _, _, rows, _ = acts.shape
    own_rows, hidden = momentum.shape[2:]
    slice_width = hidden_grad.shape[3]
    quarter = PANEL // (2 * n_tensor)
    bf16, f32 = jnp.bfloat16, jnp.float32
    vmem = pl.BlockSpec(memory_space=pltpu.VMEM)
    hbm = pl.BlockSpec(memory_space=pltpu.HBM)
    shape = jax.ShapeDtypeStruct

    in_hbm = lambda array: pltpu.with_memory_space_constraint(array, pltpu.HBM)
    deep = rows * slice_width // hidden
    in_hbm = lambda array: pltpu.with_memory_space_constraint(array, pltpu.HBM)
    deep = rows * slice_width // hidden
    piece = shape((rows, slice_width), bf16)
    outer, cross = pl.pallas_call(
        fetch,
        out_shape=(piece, piece),
        in_specs=[hbm],
        out_specs=(vmem,) * 2,
        scratch_shapes=[pltpu.SemaphoreType.DMA((2,))],
        compiler_params=pltpu.CompilerParams(vmem_limit_bytes=8 << 20),
        cost_estimate=pl.CostEstimate(flops=0, bytes_accessed=8 * rows * slice_width, transcendentals=0),
        name="fetch",
    )(in_hbm(hidden_grad))
    h2 = exchange(outer, along, 2)
    h3 = exchange(cross, diagonal, 3)
    own, window = pl.pallas_call(
        pack,
        out_shape=(shape((own_rows + deep, hidden), bf16), shape((rows, 2 * own_rows), bf16)),
        in_specs=[hbm] * 3,
        out_specs=(vmem,) * 2,
        scratch_shapes=[pltpu.SemaphoreType.DMA((2 + rows // deep,))],
        compiler_params=pltpu.CompilerParams(vmem_limit_bytes=8 << 20),
        cost_estimate=pl.CostEstimate(flops=0, bytes_accessed=8 * rows * own_rows * 2, transcendentals=0),
        name="pack",
    )(in_hbm(hidden_grad), in_hbm(acts), in_hbm(momentum))
    mate = flip(own, 0, 1)
    arrived = lax.ppermute(act_grad[0], "pipe", [(i + 1, i) for i in range(sections - 1)])
    xt = pl.pallas_call(
        prepare,
        out_shape=shape((2 * own_rows, rows), bf16),
        in_specs=[vmem, pl.BlockSpec(memory_space=pltpu.SMEM)],
        out_specs=vmem,
        compiler_params=pltpu.CompilerParams(vmem_limit_bytes=8 << 20),
        cost_estimate=pl.CostEstimate(flops=0, bytes_accessed=4 * rows * own_rows * 2, transcendentals=0),
        name="prepare",
    )(window, counts)
    block = shape((quarter, hidden), bf16)
    new, keep, near, side, far = pl.pallas_call(
        main,
        out_shape=(shape((own_rows, hidden), bf16), shape((quarter, hidden), f32), block, block, block),
        in_specs=[vmem] * 5,
        out_specs=(hbm,) + (vmem,) * 4,
        scratch_shapes=[
            pltpu.VMEM((2 * own_rows, hidden), bf16),
            pltpu.VMEM((PANEL // 2, hidden), f32),
            pltpu.SemaphoreType.DMA,
        ],
        compiler_params=pltpu.CompilerParams(vmem_limit_bytes=20 << 20),
        cost_estimate=pl.CostEstimate(
            flops=4 * own_rows * hidden * (rows + PANEL // 2),
            bytes_accessed=8 * own_rows * hidden,
            transcendentals=0,
        ),
        name="gradients",
    )(xt, own, h2, h3, mate)
    far = flip(far, 1, 2)
    side = flip(side, 1, 0)
    near = flip(near, 0, 2)
    gram, received = pl.pallas_call(
        finish,
        out_shape=(shape((quarter, hidden), f32), shape(arrived.shape, bf16)),
        in_specs=[vmem] * 4 + [pl.BlockSpec(memory_space=pl.ANY)],
        out_specs=(hbm, hbm),
        scratch_shapes=[pltpu.VMEM((quarter, hidden), f32), pltpu.SemaphoreType.DMA((2,))],
        compiler_params=pltpu.CompilerParams(vmem_limit_bytes=8 << 20),
        cost_estimate=pl.CostEstimate(flops=0, bytes_accessed=20 * quarter * hidden, transcendentals=0),
        name="finish",
    )(keep, near, side, far, arrived)
    return new[None, None], gram[None, None], received[None]


def solution(mesh):
    return jax.shard_map(
        on_device,
        mesh=mesh,
        in_specs=(
            P("pipe", "expert", None, None),
            P("pipe", None, None, "tensor"),
            P("pipe", None, None),
            P("pipe", "expert", "tensor", None),
            P("pipe", "expert", "tensor"),
        ),
        out_specs=(
            P("pipe", "expert", "tensor", None),
            P("pipe", "expert", "tensor", None),
            P("pipe", "expert", "tensor"),
        ),
        check_vma=False,
    )
```

time: 51.4 us -> 49.8 us (0.969)
  waiting for transfers between devices: 13 us -> 11.7 us
  starting transfers between devices: 32 us -> 31.1 us
  Pallas kernels: 5.15 us -> 5.74 us
    ppermute x6 -> x4, starting transfers between devices: 28.8 us -> 21.3 us  [flip(): return lax.ppermute(array, ('expert', 'tensor'), route)]
    ppermute x1 -> x2, starting transfers between devices: 1.92 us -> 8.49 us  [exchange(): return lax.ppermute(array, ('expert', 'tensor'), route)]
    ppermute x1 -> x2, waiting for transfers between devices: 3.45 us -> 1.36 us  [exchange(): return lax.ppermute(array, ('expert', 'tensor'), route)]
    pallas_call x1 -> x2, Pallas kernels: 1.2 us -> 2.43 us  [the longest x1 1.41 us: on_device(): pl.pallas_call(pack, out_shape=(shape((own_rows + deep, hidden), bf16), s...]
    ppermute x6 -> x4, waiting for transfers between devices: 9.59 us -> 10.3 us  [flip(): return lax.ppermute(array, ('expert', 'tensor'), route)]
    pallas_call x1, Pallas kernels: 1.4 us -> 0.79 us  [on_device(): pl.pallas_call(finish, out_shape=(shape((quarter, hidden), f32), shape(ar...]
  transfers between devices with their start and end apart: 8 -> 7, of which waited for: 3 -> 3; matrix products, arithmetic and copies ran while one was open for 0% -> 0% of each run, Pallas kernels for 7% -> 7%
where the time goes in v1:
time: 49.8 us; the launch traced here: 49.4 us
  starting transfers between devices  31.1 us (62%)
  waiting for transfers between devices  11.7 us (23%)
  Pallas kernels  5.74 us (12%)
  between operations  0.77 us (2%)
    ppermute x4, starting transfers between devices, flip(): return lax.ppermute(array, ('expert', 'tensor'), route)  21.3 us
    ppermute x4, waiting for transfers between devices, flip(): return lax.ppermute(array, ('expert', 'tensor'), route)  10.3 us
    ppermute x2, starting transfers between devices, exchange(): return lax.ppermute(array, ('expert', 'tensor'), route)  8.49 us
    pallas_call x1, Pallas kernels, on_device(): pl.pallas_call(main, out_shape=(shape((own_rows, hidden), bf16), shape((q...  1.73 us
    pallas_call x1, Pallas kernels, on_device(): pl.pallas_call(pack, out_shape=(shape((own_rows + deep, hidden), bf16), s...  1.41 us
    ppermute x2, waiting for transfers between devices, exchange(): return lax.ppermute(array, ('expert', 'tensor'), route)  1.36 us
    ppermute x1, starting transfers between devices, on_device(): lax.ppermute(act_grad[0], 'pipe', [(i + 1, i) for i in range(sections - 1)])  1.29 us
    pallas_call x1, Pallas kernels, on_device(): pl.pallas_call(fetch, out_shape=(piece, piece), in_specs=[hbm], out_specs...  1.02 us
  transfers between devices with their start and end apart: 7, of which 3 were waited for; matrix products, arithmetic and copies ran while one was open for 0% of the time, Pallas kernels for 7%

profile of v1, /device:TPU:8, one launch (start us, length us, event | category | flops | bytes accessed | tf_op | source)
XLA Modules:
  0.0 49.4 jit_solution(9576518899287346304)
XLA Ops:
  0.6 1.4 %pack.1 = (bf16[512,1024]{1,0:T(8,128)(2,1)S(1)}, bf16[256,896]{1,0:T(8,128)(2,1)S(1)}) custom-call(bf16[1,8,256,256]{3,2,1,0:T(8,128)(2,1)} %grad_ref.3, bf16[1,1,256,1792]{3,2,1,0:T(8,128)(2,1)} %acts_ref.1, bf16[1,1,448,1024]{3,2,1,0:T(8,128)(2,1)} %moment_ref.1), custom_call_target="tpu_custom_call" | custom-call | bytes 1835008 | tf_op jit(solution)/shard_map/pack/pallas_call | solution.py:153
  2.0 0.0 copy-start.1
  2.1 2.1 %collective-permute-start.2 = (bf16[512,1024]{1,0:T(8,128)(2,1)S(1)}, bf16[512,1024]{1,0:T(8,128)(2,1)S(1)}, u32[]{:S(2)}, u32[]{:S(2)}) collective-permute-start(bf16[512,1024]{1,0:T(8,128)(2,1)S(1)} %get-tuple-element.15.own_ref), channel_id=1, source_target_pairs={{0,1},{1,0},{2,3},{3,2},{4,5},{5,4},{6,7},{7,6},{8,9},{9,8},{10,11... | collective-permute-start | bytes 3145736 | tf_op jit(solution)/shard_map/ppermute | solution.py:115
  4.1 1.0 %fetch.1 = (bf16[256,256]{1,0:T(8,128)(2,1)S(1)}, bf16[256,256]{1,0:T(8,128)(2,1)S(1)}) custom-call(bf16[1,8,256,256]{3,2,1,0:T(8,128)(2,1)} %grad_ref.3), custom_call_target="tpu_custom_call" | custom-call | bytes 524288 | tf_op jit(solution)/shard_map/fetch/pallas_call | solution.py:141
  5.1 3.5 %collective-permute-start = (bf16[256,256]{1,0:T(8,128)(2,1)S(1)}, bf16[256,256]{1,0:T(8,128)(2,1)S(1)}, u32[]{:S(2)}, u32[]{:S(2)}) collective-permute-start(bf16[256,256]{1,0:T(8,128)(2,1)S(1)} %get-tuple-element.16), channel_id=1, source_target_pairs={{0,14},{1,15},{2,4},{3,5},{4,2},{5,3},{6,8},{7,9},{8,6},{9,7},{10,... | collective-permute-start | bytes 393224 | tf_op jit(solution)/shard_map/ppermute | solution.py:121
  8.6 0.0 copy-start
  8.7 5.0 %collective-permute-start.1 = (bf16[256,256]{1,0:T(8,128)(2,1)S(1)}, bf16[256,256]{1,0:T(8,128)(2,1)S(1)}, u32[]{:S(2)}, u32[]{:S(2)}) collective-permute-start(bf16[256,256]{1,0:T(8,128)(2,1)S(1)} %get-tuple-element.17), channel_id=1, source_target_pairs={{0,51},{1,50},{2,17},{3,16},{4,55},{5,54},{6,21},{7,20},{8,59},{9,... | collective-permute-start | bytes 393224 | tf_op jit(solution)/shard_map/ppermute | solution.py:121
  13.7 0.0 copy-done.1
  13.7 1.3 %collective-permute-start.6 = (bf16[64,1792]{1,0:T(8,128)(2,1)S(1)}, bf16[64,1792]{1,0:T(8,128)(2,1)S(1)}, u32[]{:S(2)}, u32[]{:S(2)}) collective-permute-start(bf16[64,1792]{1,0:T(8,128)(2,1)S(1)} %bitcast.5), channel_id=1, source_target_pairs={{64,0},{128,64},{192,128},{256,192},{320,256},{384,320},{448,384},... | collective-permute-start | bytes 688136 | tf_op jit(solution)/shard_map/ppermute | solution.py:164
  15.0 0.0 copy-done
  15.0 0.1 copy.8.counts_ref
  15.1 0.8 %prepare.1.xt_ref = bf16[896,256]{1,0:T(8,128)(2,1)S(1)} custom-call(bf16[256,896]{1,0:T(8,128)(2,1)S(1)} %get-tuple-element.14.window_ref, s32[1,8,2]{2,1,0:T(8,128)S(1)} %copy.8.counts_ref), custom_call_target="tpu_custom_call" | custom-call | bytes 917504 | tf_op jit(solution)/shard_map/prepare/pallas_call | solution.py:165
  15.9 0.0 collective-permute-done.h2
  15.9 1.4 %collective-permute-done.1.h3 = bf16[256,256]{1,0:T(8,128)(2,1)S(1)} collective-permute-done((bf16[256,256]{1,0:T(8,128)(2,1)S(1)}, bf16[256,256]{1,0:T(8,128)(2,1)S(1)}, u32[]{:S(2)}, u32[]{:S(2)}) %collective-permute-start.1) | collective-permute-done | bytes 131104 | tf_op jit(solution)/shard_map/ppermute | solution.py:121
  17.2 0.0 collective-permute-done.2.mate_ref
  17.2 1.7 %gradients.1 = (bf16[448,1024]{1,0:T(8,128)(2,1)}, f32[64,1024]{1,0:T(8,128)S(1)}, bf16[64,1024]{1,0:T(8,128)(2,1)S(1)}, bf16[64,1024]{1,0:T(8,128)(2,1)S(1)}, bf16[64,1024]{1,0:T(8,128)(2,1)S(1)}) custom-call(bf16[896,256]{1,0:T(8,128)(2,1)S(1)} %prepare.1.xt_ref, bf16[512,1024]{1,0:T(8,128)(2,1)S(1)} %get-tuple-element.15.own_ref, ...), custom_call_target="tpu_custom_call" | custom-call | flops 939524096 | bytes 3670016 | tf_op jit(solution)/shard_map/gradients/pallas_call | solution.py:175
  19.0 14.0 %collective-permute-start.3 = (bf16[64,1024]{1,0:T(8,128)(2,1)S(1)}, bf16[64,1024]{1,0:T(8,128)(2,1)S(1)}, u32[]{:S(2)}, u32[]{:S(2)}) collective-permute-start(bf16[64,1024]{1,0:T(8,128)(2,1)S(1)} %get-tuple-element.20), channel_id=1, source_target_pairs={{0,2},{1,3},{2,0},{3,1},{4,6},{5,7},{6,4},{7,5},{8,10},{9,11},{10,... | collective-permute-start | bytes 393224 | tf_op jit(solution)/shard_map/ppermute | solution.py:115
  33.0 1.9 %collective-permute-start.4 = (bf16[64,1024]{1,0:T(8,128)(2,1)S(1)}, bf16[64,1024]{1,0:T(8,128)(2,1)S(1)}, u32[]{:S(2)}, u32[]{:S(2)}) collective-permute-start(bf16[64,1024]{1,0:T(8,128)(2,1)S(1)} %get-tuple-element.21), channel_id=1, source_target_pairs={{0,4},{1,5},{2,6},{3,7},{4,0},{5,1},{6,2},{7,3},{8,12},{9,13},{10,... | collective-permute-start | bytes 393224 | tf_op jit(solution)/shard_map/ppermute | solution.py:115
  34.9 3.4 %collective-permute-start.5 = (bf16[64,1024]{1,0:T(8,128)(2,1)S(1)}, bf16[64,1024]{1,0:T(8,128)(2,1)S(1)}, u32[]{:S(2)}, u32[]{:S(2)}) collective-permute-start(bf16[64,1024]{1,0:T(8,128)(2,1)S(1)} %get-tuple-element.22), channel_id=1, source_target_pairs={{0,6},{1,7},{2,4},{3,5},{4,2},{5,3},{6,0},{7,1},{8,14},{9,15},{10,... | collective-permute-start | bytes 393224 | tf_op jit(solution)/shard_map/ppermute | solution.py:115
  38.3 0.0 collective-permute-done.6.arrived_ref
  38.3 0.0 collective-permute-done.3.near_ref
  38.3 5.9 %collective-permute-done.4.side_ref = bf16[64,1024]{1,0:T(8,128)(2,1)S(1)} collective-permute-done((bf16[64,1024]{1,0:T(8,128)(2,1)S(1)}, bf16[64,1024]{1,0:T(8,128)(2,1)S(1)}, u32[]{:S(2)}, u32[]{:S(2)}) %collective-permute-start.4) | collective-permute-done | bytes 131104 | tf_op jit(solution)/shard_map/ppermute | solution.py:115
  44.2 4.4 %collective-permute-done.5.far_ref = bf16[64,1024]{1,0:T(8,128)(2,1)S(1)} collective-permute-done((bf16[64,1024]{1,0:T(8,128)(2,1)S(1)}, bf16[64,1024]{1,0:T(8,128)(2,1)S(1)}, u32[]{:S(2)}, u32[]{:S(2)}) %collective-permute-start.5) | collective-permute-done | bytes 131104 | tf_op jit(solution)/shard_map/ppermute | solution.py:115
  48.6 0.8 %finish.1 = (f32[64,1024]{1,0:T(8,128)}, bf16[64,1792]{1,0:T(8,128)(2,1)}) custom-call(f32[64,1024]{1,0:T(8,128)S(1)} %get-tuple-element.19.keep_ref, bf16[64,1024]{1,0:T(8,128)(2,1)S(1)} %collective-permute-done.3.near_ref, bf16[64,1024]{1,0:T(8,128)(2,1)S(1)} %collective-permute-done.4.side_ref, bf16[64,1024]{1,0:T(8,128)(2,1)S(1)} %collective-permute-done.5.far_ref, ...), custom_call_target="tpu_custom_call" | custom-call | bytes 1310720 | tf_op jit(solution)/shard_map/finish/pallas_call | solution.py:196
Async XLA Ops:
  2.0 11.6 %copy-start.1 = (bf16[1,64,1792]{2,1,0:T(8,128)(2,1)S(1)}, bf16[1,64,1792]{2,1,0:T(8,128)(2,1)}, u32[]{:S(2)}) copy-start(bf16[1,64,1792]{2,1,0:T(8,128)(2,1)} %param.9) | copy-start | bytes 688132
  2.1 15.2 %collective-permute-start.2 = (bf16[512,1024]{1,0:T(8,128)(2,1)S(1)}, bf16[512,1024]{1,0:T(8,128)(2,1)S(1)}, u32[]{:S(2)}, u32[]{:S(2)}) collective-permute-start(bf16[512,1024]{1,0:T(8,128)(2,1)S(1)} %get-tuple-element.15.own_ref), channel_id=1, source_target_pairs={{0,1},{1,0},{2,3},{3,2},{4,5},{5,4},{6,7},{7,6},{8,9},{9,8},{10,11... | collective-permute-start | bytes 3145736 | tf_op jit(solution)/shard_map/ppermute | solution.py:115
  5.1 10.7 %collective-permute-start = (bf16[256,256]{1,0:T(8,128)(2,1)S(1)}, bf16[256,256]{1,0:T(8,128)(2,1)S(1)}, u32[]{:S(2)}, u32[]{:S(2)}) collective-permute-start(bf16[256,256]{1,0:T(8,128)(2,1)S(1)} %get-tuple-element.16), channel_id=1, source_target_pairs={{0,14},{1,15},{2,4},{3,5},{4,2},{5,3},{6,8},{7,9},{8,6},{9,7},{10,... | collective-permute-start | bytes 393224 | tf_op jit(solution)/shard_map/ppermute | solution.py:121
  8.6 6.3 %copy-start = (s32[1,8,2]{1,2,0:T(2,128)S(1)}, s32[1,8,2]{1,2,0:T(2,128)}, u32[]{:S(2)}) copy-start(s32[1,8,2]{1,2,0:T(2,128)} %param.7) | copy-start | bytes 196
  8.7 8.6 %collective-permute-start.1 = (bf16[256,256]{1,0:T(8,128)(2,1)S(1)}, bf16[256,256]{1,0:T(8,128)(2,1)S(1)}, u32[]{:S(2)}, u32[]{:S(2)}) collective-permute-start(bf16[256,256]{1,0:T(8,128)(2,1)S(1)} %get-tuple-element.17), channel_id=1, source_target_pairs={{0,51},{1,50},{2,17},{3,16},{4,55},{5,54},{6,21},{7,20},{8,59},{9,... | collective-permute-start | bytes 393224 | tf_op jit(solution)/shard_map/ppermute | solution.py:121
  13.7 24.6 %collective-permute-start.6 = (bf16[64,1792]{1,0:T(8,128)(2,1)S(1)}, bf16[64,1792]{1,0:T(8,128)(2,1)S(1)}, u32[]{:S(2)}, u32[]{:S(2)}) collective-permute-start(bf16[64,1792]{1,0:T(8,128)(2,1)S(1)} %bitcast.5), channel_id=1, source_target_pairs={{64,0},{128,64},{192,128},{256,192},{320,256},{384,320},{448,384},... | collective-permute-start | bytes 688136 | tf_op jit(solution)/shard_map/ppermute | solution.py:164
  19.0 19.3 %collective-permute-start.3 = (bf16[64,1024]{1,0:T(8,128)(2,1)S(1)}, bf16[64,1024]{1,0:T(8,128)(2,1)S(1)}, u32[]{:S(2)}, u32[]{:S(2)}) collective-permute-start(bf16[64,1024]{1,0:T(8,128)(2,1)S(1)} %get-tuple-element.20), channel_id=1, source_target_pairs={{0,2},{1,3},{2,0},{3,1},{4,6},{5,7},{6,4},{7,5},{8,10},{9,11},{10,... | collective-permute-start | bytes 393224 | tf_op jit(solution)/shard_map/ppermute | solution.py:115
  33.0 11.2 %collective-permute-start.4 = (bf16[64,1024]{1,0:T(8,128)(2,1)S(1)}, bf16[64,1024]{1,0:T(8,128)(2,1)S(1)}, u32[]{:S(2)}, u32[]{:S(2)}) collective-permute-start(bf16[64,1024]{1,0:T(8,128)(2,1)S(1)} %get-tuple-element.21), channel_id=1, source_target_pairs={{0,4},{1,5},{2,6},{3,7},{4,0},{5,1},{6,2},{7,3},{8,12},{9,13},{10,... | collective-permute-start | bytes 393224 | tf_op jit(solution)/shard_map/ppermute | solution.py:115
  34.9 13.7 %collective-permute-start.5 = (bf16[64,1024]{1,0:T(8,128)(2,1)S(1)}, bf16[64,1024]{1,0:T(8,128)(2,1)S(1)}, u32[]{:S(2)}, u32[]{:S(2)}) collective-permute-start(bf16[64,1024]{1,0:T(8,128)(2,1)S(1)} %get-tuple-element.22), channel_id=1, source_target_pairs={{0,6},{1,7},{2,4},{3,5},{4,2},{5,3},{6,0},{7,1},{8,14},{9,15},{10,... | collective-permute-start | bytes 393224 | tf_op jit(solution)/shard_map/ppermute | solution.py:115

commit v2 on v1

--- a/solution.py
+++ b/solution.py
@@ -12,34 +12,27 @@
 DECAY = 0.9
 
 
-def run_copies(moves, sems):
-    copies = [pltpu.make_async_copy(source, target, sems.at[i]) for i, (source, target) in enumerate(moves)]
-    for copy in copies:
-        copy.start()
-    for copy in copies:
-        copy.wait()
-
-
-def fetch(grad_ref, outer_ref, cross_ref, sems):
-    t, e = lax.axis_index("tensor"), lax.axis_index("expert")
-    run_copies(
-        [(grad_ref.at[0, along(e, t) // 2], outer_ref), (grad_ref.at[0, diagonal(e, t) // 2], cross_ref)], sems
-    )
-
-
-def pack(grad_ref, acts_ref, moment_ref, packed_ref, window_ref, sems):
+def fetch(grad_ref, acts_ref, moment_ref, packed_ref, outer_ref, cross_ref, window_ref, sems):
     t, e = lax.axis_index("tensor"), lax.axis_index("expert")
     width = window_ref.shape[1]
     start = pl.multiple_of(t // 2 * width, 128)
     rows = moment_ref.shape[2]
     deep, wide = packed_ref.shape[0] - rows, grad_ref.shape[3]
-    moves = [(moment_ref.at[0, 0], packed_ref.at[pl.ds(0, rows)])]
+    moves = [
+        (grad_ref.at[0, (e ^ Y_HI) // 2], cross_ref),
+        (grad_ref.at[0, along(e, t) // 2], outer_ref),
+        (moment_ref.at[0, 0], packed_ref.at[pl.ds(0, rows)]),
+    ]
     for k in range(packed_ref.shape[1] // wide):
         moves.append(
             (grad_ref.at[0, e // 2, pl.ds(k * deep, deep)], packed_ref.at[pl.ds(rows, deep), pl.ds(k * wide, wide)])
         )
     moves.append((acts_ref.at[0, 0, :, pl.ds(start, width)], window_ref))
-    run_copies(moves, sems)
+    copies = [pltpu.make_async_copy(a, b, sems.at[i]) for i, (a, b) in enumerate(moves)]
+    for copy in copies:
+        copy.start()
+    for copy in copies:
+        copy.wait()
 
 
 def prepare(window_ref, counts_ref, xt_ref):
@@ -102,11 +95,6 @@
     return e // Y_HI * Y_HI + (e % Y_HI + (t // 2 * 2 - 1) + Y_HI) % Y_HI
 
 
-def diagonal(e, t):
-    count = lax.axis_size("expert")
-    return (e + (t // 2 * 2 - 1) * Y_HI + count) % count
-
-
 def flip(array, expert_bit, tensor_bits):
     ne, nt = lax.axis_size("expert"), lax.axis_size("tensor")
     route = [
@@ -135,31 +123,23 @@
 
     in_hbm = lambda array: pltpu.with_memory_space_constraint(array, pltpu.HBM)
     deep = rows * slice_width // hidden
-    in_hbm = lambda array: pltpu.with_memory_space_constraint(array, pltpu.HBM)
-    deep = rows * slice_width // hidden
-    piece = shape((rows, slice_width), bf16)
-    outer, cross = pl.pallas_call(
+    own, outer, cross, window = pl.pallas_call(
         fetch,
-        out_shape=(piece, piece),
-        in_specs=[hbm],
-        out_specs=(vmem,) * 2,
-        scratch_shapes=[pltpu.SemaphoreType.DMA((2,))],
-        compiler_params=pltpu.CompilerParams(vmem_limit_bytes=8 << 20),
-        cost_estimate=pl.CostEstimate(flops=0, bytes_accessed=8 * rows * slice_width, transcendentals=0),
-        name="fetch",
-    )(in_hbm(hidden_grad))
-    h2 = exchange(outer, along, 2)
-    h3 = exchange(cross, diagonal, 3)
-    own, window = pl.pallas_call(
-        pack,
-        out_shape=(shape((own_rows + deep, hidden), bf16), shape((rows, 2 * own_rows), bf16)),
+        out_shape=(
+            shape((own_rows + deep, hidden), bf16),
+            shape((rows, slice_width), bf16),
+            shape((rows, slice_width), bf16),
+            shape((rows, 2 * own_rows), bf16),
+        ),
         in_specs=[hbm] * 3,
-        out_specs=(vmem,) * 2,
-        scratch_shapes=[pltpu.SemaphoreType.DMA((2 + rows // deep,))],
+        out_specs=(vmem,) * 4,
+        scratch_shapes=[pltpu.SemaphoreType.DMA((4 + rows // deep,))],
         compiler_params=pltpu.CompilerParams(vmem_limit_bytes=8 << 20),
         cost_estimate=pl.CostEstimate(flops=0, bytes_accessed=8 * rows * own_rows * 2, transcendentals=0),
-        name="pack",
+        name="fetch",
     )(in_hbm(hidden_grad), in_hbm(acts), in_hbm(momentum))
+    h3 = flip(cross, Y_HI, 3)
+    h2 = exchange(outer, along, 2)
     mate = flip(own, 0, 1)
     arrived = lax.ppermute(act_grad[0], "pipe", [(i + 1, i) for i in range(sections - 1)])
     xt = pl.pallas_call(

time: 49.8 us -> 47.6 us (0.956)
  the two profiles are of different devices: /device:TPU:8 before, /device:TPU:48 now
where the time goes in v2:
time: 47.6 us; the launch traced here: 47.3 us
  starting transfers between devices  27.7 us (58%)
  waiting for transfers between devices  13.8 us (29%)
  Pallas kernels  4.95 us (10%)
  between operations  0.76 us (2%)
    ppermute x5, starting transfers between devices, flip(): return lax.ppermute(array, ('expert', 'tensor'), route)  23.1 us
    ppermute x5, waiting for transfers between devices, flip(): return lax.ppermute(array, ('expert', 'tensor'), route)  13.8 us
    ppermute x1, starting transfers between devices, exchange(): return lax.ppermute(array, ('expert', 'tensor'), route)  3.26 us
    pallas_call x1, Pallas kernels, on_device(): pl.pallas_call(main, out_shape=(shape((own_rows, hidden), bf16), shape((q...  1.74 us
    pallas_call x1, Pallas kernels, on_device(): pl.pallas_call(fetch, out_shape=(shape((own_rows + deep, hidden), bf16),...  1.62 us
    ppermute x1, starting transfers between devices, on_device(): lax.ppermute(act_grad[0], 'pipe', [(i + 1, i) for i in range(sections - 1)])  1.29 us
  transfers between devices with their start and end apart: 7, of which 3 were waited for; matrix products, arithmetic and copies ran while one was open for 0% of the time, Pallas kernels for 5%

profile of v2, /device:TPU:48, one launch (start us, length us, event | category | flops | bytes accessed | tf_op | source)
XLA Modules:
  0.0 47.3 jit_solution(15041233364282405070)
XLA Ops:
  0.6 0.0 copy-start.1
  0.6 1.6 %fetch.1 = (bf16[512,1024]{1,0:T(8,128)(2,1)S(1)}, bf16[256,256]{1,0:T(8,128)(2,1)S(1)}, bf16[256,256]{1,0:T(8,128)(2,1)S(1)}, bf16[256,896]{1,0:T(8,128)(2,1)S(1)}) custom-call(bf16[1,8,256,256]{3,2,1,0:T(8,128)(2,1)} %grad_ref.1, bf16[1,1,256,1792]{3,2,1,0:T(8,128)(2,1)} %acts_ref.1, bf16[1,1,448,1024]{3,2,1,0:T(8,128)(2,1)} %moment_ref.1), custom_call_target="tpu_custom_call" | custom-call | bytes 1835008 | tf_op jit(solution)/shard_map/fetch/pallas_call | solution.py:126
  2.3 1.9 %collective-permute-start.2 = (bf16[512,1024]{1,0:T(8,128)(2,1)S(1)}, bf16[512,1024]{1,0:T(8,128)(2,1)S(1)}, u32[]{:S(2)}, u32[]{:S(2)}) collective-permute-start(bf16[512,1024]{1,0:T(8,128)(2,1)S(1)} %get-tuple-element.15.own_ref), channel_id=1, source_target_pairs={{0,1},{1,0},{2,3},{3,2},{4,5},{5,4},{6,7},{7,6},{8,9},{9,8},{10,11... | collective-permute-start | bytes 3145736 | tf_op jit(solution)/shard_map/ppermute | solution.py:103
  4.2 3.3 %collective-permute-start = (bf16[256,256]{1,0:T(8,128)(2,1)S(1)}, bf16[256,256]{1,0:T(8,128)(2,1)S(1)}, u32[]{:S(2)}, u32[]{:S(2)}) collective-permute-start(bf16[256,256]{1,0:T(8,128)(2,1)S(1)} %get-tuple-element.16), channel_id=1, source_target_pairs={{0,14},{1,15},{2,4},{3,5},{4,2},{5,3},{6,8},{7,9},{8,6},{9,7},{10,... | collective-permute-start | bytes 393224 | tf_op jit(solution)/shard_map/ppermute | solution.py:109
  7.5 0.0 copy-start
  7.5 2.3 %collective-permute-start.1 = (bf16[256,256]{1,0:T(8,128)(2,1)S(1)}, bf16[256,256]{1,0:T(8,128)(2,1)S(1)}, u32[]{:S(2)}, u32[]{:S(2)}) collective-permute-start(bf16[256,256]{1,0:T(8,128)(2,1)S(1)} %get-tuple-element.17), channel_id=1, source_target_pairs={{0,19},{1,18},{2,17},{3,16},{4,23},{5,22},{6,21},{7,20},{8,27},{9,... | collective-permute-start | bytes 393224 | tf_op jit(solution)/shard_map/ppermute | solution.py:103
  9.8 0.0 copy-done.1
  9.8 1.3 %collective-permute-start.6 = (bf16[64,1792]{1,0:T(8,128)(2,1)S(1)}, bf16[64,1792]{1,0:T(8,128)(2,1)S(1)}, u32[]{:S(2)}, u32[]{:S(2)}) collective-permute-start(bf16[64,1792]{1,0:T(8,128)(2,1)S(1)} %bitcast.5), channel_id=1, source_target_pairs={{64,0},{128,64},{192,128},{256,192},{320,256},{384,320},{448,384},... | collective-permute-start | bytes 688136 | tf_op jit(solution)/shard_map/ppermute | solution.py:144
  11.1 0.0 copy-done
  11.1 0.1 copy.8.counts_ref
  11.2 0.8 %prepare.1.xt_ref = bf16[896,256]{1,0:T(8,128)(2,1)S(1)} custom-call(bf16[256,896]{1,0:T(8,128)(2,1)S(1)} %get-tuple-element.14.window_ref, s32[1,8,2]{2,1,0:T(8,128)S(1)} %copy.8.counts_ref), custom_call_target="tpu_custom_call" | custom-call | bytes 917504 | tf_op jit(solution)/shard_map/prepare/pallas_call | solution.py:145
  12.0 0.0 collective-permute-done.h2
  12.0 3.7 %collective-permute-done.1.h3 = bf16[256,256]{1,0:T(8,128)(2,1)S(1)} collective-permute-done((bf16[256,256]{1,0:T(8,128)(2,1)S(1)}, bf16[256,256]{1,0:T(8,128)(2,1)S(1)}, u32[]{:S(2)}, u32[]{:S(2)}) %collective-permute-start.1) | collective-permute-done | bytes 131104 | tf_op jit(solution)/shard_map/ppermute | solution.py:103
  15.7 0.0 collective-permute-done.2.mate_ref
  15.7 1.7 %gradients.1 = (bf16[448,1024]{1,0:T(8,128)(2,1)}, f32[64,1024]{1,0:T(8,128)S(1)}, bf16[64,1024]{1,0:T(8,128)(2,1)S(1)}, bf16[64,1024]{1,0:T(8,128)(2,1)S(1)}, bf16[64,1024]{1,0:T(8,128)(2,1)S(1)}) custom-call(bf16[896,256]{1,0:T(8,128)(2,1)S(1)} %prepare.1.xt_ref, bf16[512,1024]{1,0:T(8,128)(2,1)S(1)} %get-tuple-element.15.own_ref, ...), custom_call_target="tpu_custom_call" | custom-call | flops 939524096 | bytes 3670016 | tf_op jit(solution)/shard_map/gradients/pallas_call | solution.py:155
  17.4 13.6 %collective-permute-start.3 = (bf16[64,1024]{1,0:T(8,128)(2,1)S(1)}, bf16[64,1024]{1,0:T(8,128)(2,1)S(1)}, u32[]{:S(2)}, u32[]{:S(2)}) collective-permute-start(bf16[64,1024]{1,0:T(8,128)(2,1)S(1)} %get-tuple-element.20), channel_id=1, source_target_pairs={{0,2},{1,3},{2,0},{3,1},{4,6},{5,7},{6,4},{7,5},{8,10},{9,11},{10,... | collective-permute-start | bytes 393224 | tf_op jit(solution)/shard_map/ppermute | solution.py:103
  31.0 1.9 %collective-permute-start.4 = (bf16[64,1024]{1,0:T(8,128)(2,1)S(1)}, bf16[64,1024]{1,0:T(8,128)(2,1)S(1)}, u32[]{:S(2)}, u32[]{:S(2)}) collective-permute-start(bf16[64,1024]{1,0:T(8,128)(2,1)S(1)} %get-tuple-element.21), channel_id=1, source_target_pairs={{0,4},{1,5},{2,6},{3,7},{4,0},{5,1},{6,2},{7,3},{8,12},{9,13},{10,... | collective-permute-start | bytes 393224 | tf_op jit(solution)/shard_map/ppermute | solution.py:103
  33.0 3.4 %collective-permute-start.5 = (bf16[64,1024]{1,0:T(8,128)(2,1)S(1)}, bf16[64,1024]{1,0:T(8,128)(2,1)S(1)}, u32[]{:S(2)}, u32[]{:S(2)}) collective-permute-start(bf16[64,1024]{1,0:T(8,128)(2,1)S(1)} %get-tuple-element.22), channel_id=1, source_target_pairs={{0,6},{1,7},{2,4},{3,5},{4,2},{5,3},{6,0},{7,1},{8,14},{9,15},{10,... | collective-permute-start | bytes 393224 | tf_op jit(solution)/shard_map/ppermute | solution.py:103
  36.4 0.0 collective-permute-done.6.arrived_ref
  36.4 0.0 collective-permute-done.3.near_ref
  36.4 5.7 %collective-permute-done.4.side_ref = bf16[64,1024]{1,0:T(8,128)(2,1)S(1)} collective-permute-done((bf16[64,1024]{1,0:T(8,128)(2,1)S(1)}, bf16[64,1024]{1,0:T(8,128)(2,1)S(1)}, u32[]{:S(2)}, u32[]{:S(2)}) %collective-permute-start.4) | collective-permute-done | bytes 131104 | tf_op jit(solution)/shard_map/ppermute | solution.py:103
  42.0 4.4 %collective-permute-done.5.far_ref = bf16[64,1024]{1,0:T(8,128)(2,1)S(1)} collective-permute-done((bf16[64,1024]{1,0:T(8,128)(2,1)S(1)}, bf16[64,1024]{1,0:T(8,128)(2,1)S(1)}, u32[]{:S(2)}, u32[]{:S(2)}) %collective-permute-start.5) | collective-permute-done | bytes 131104 | tf_op jit(solution)/shard_map/ppermute | solution.py:103
  46.5 0.8 %finish.1 = (f32[64,1024]{1,0:T(8,128)}, bf16[64,1792]{1,0:T(8,128)(2,1)}) custom-call(f32[64,1024]{1,0:T(8,128)S(1)} %get-tuple-element.19.keep_ref, bf16[64,1024]{1,0:T(8,128)(2,1)S(1)} %collective-permute-done.3.near_ref, bf16[64,1024]{1,0:T(8,128)(2,1)S(1)} %collective-permute-done.4.side_ref, bf16[64,1024]{1,0:T(8,128)(2,1)S(1)} %collective-permute-done.5.far_ref, ...), custom_call_target="tpu_custom_call" | custom-call | bytes 1310720 | tf_op jit(solution)/shard_map/finish/pallas_call | solution.py:176
Async XLA Ops:
  0.6 9.1 %copy-start.1 = (bf16[1,64,1792]{2,1,0:T(8,128)(2,1)S(1)}, bf16[1,64,1792]{2,1,0:T(8,128)(2,1)}, u32[]{:S(2)}) copy-start(bf16[1,64,1792]{2,1,0:T(8,128)(2,1)} %param.9) | copy-start | bytes 688132
  2.3 13.4 %collective-permute-start.2 = (bf16[512,1024]{1,0:T(8,128)(2,1)S(1)}, bf16[512,1024]{1,0:T(8,128)(2,1)S(1)}, u32[]{:S(2)}, u32[]{:S(2)}) collective-permute-start(bf16[512,1024]{1,0:T(8,128)(2,1)S(1)} %get-tuple-element.15.own_ref), channel_id=1, source_target_pairs={{0,1},{1,0},{2,3},{3,2},{4,5},{5,4},{6,7},{7,6},{8,9},{9,8},{10,11... | collective-permute-start | bytes 3145736 | tf_op jit(solution)/shard_map/ppermute | solution.py:103
  4.2 7.8 %collective-permute-start = (bf16[256,256]{1,0:T(8,128)(2,1)S(1)}, bf16[256,256]{1,0:T(8,128)(2,1)S(1)}, u32[]{:S(2)}, u32[]{:S(2)}) collective-permute-start(bf16[256,256]{1,0:T(8,128)(2,1)S(1)} %get-tuple-element.16), channel_id=1, source_target_pairs={{0,14},{1,15},{2,4},{3,5},{4,2},{5,3},{6,8},{7,9},{8,6},{9,7},{10,... | collective-permute-start | bytes 393224 | tf_op jit(solution)/shard_map/ppermute | solution.py:109
  7.5 3.6 %copy-start = (s32[1,8,2]{1,2,0:T(2,128)S(1)}, s32[1,8,2]{1,2,0:T(2,128)}, u32[]{:S(2)}) copy-start(s32[1,8,2]{1,2,0:T(2,128)} %param.7) | copy-start | bytes 196
  7.5 8.2 %collective-permute-start.1 = (bf16[256,256]{1,0:T(8,128)(2,1)S(1)}, bf16[256,256]{1,0:T(8,128)(2,1)S(1)}, u32[]{:S(2)}, u32[]{:S(2)}) collective-permute-start(bf16[256,256]{1,0:T(8,128)(2,1)S(1)} %get-tuple-element.17), channel_id=1, source_target_pairs={{0,19},{1,18},{2,17},{3,16},{4,23},{5,22},{6,21},{7,20},{8,27},{9,... | collective-permute-start | bytes 393224 | tf_op jit(solution)/shard_map/ppermute | solution.py:103
  9.8 26.6 %collective-permute-start.6 = (bf16[64,1792]{1,0:T(8,128)(2,1)S(1)}, bf16[64,1792]{1,0:T(8,128)(2,1)S(1)}, u32[]{:S(2)}, u32[]{:S(2)}) collective-permute-start(bf16[64,1792]{1,0:T(8,128)(2,1)S(1)} %bitcast.5), channel_id=1, source_target_pairs={{64,0},{128,64},{192,128},{256,192},{320,256},{384,320},{448,384},... | collective-permute-start | bytes 688136 | tf_op jit(solution)/shard_map/ppermute | solution.py:144
  17.4 18.9 %collective-permute-start.3 = (bf16[64,1024]{1,0:T(8,128)(2,1)S(1)}, bf16[64,1024]{1,0:T(8,128)(2,1)S(1)}, u32[]{:S(2)}, u32[]{:S(2)}) collective-permute-start(bf16[64,1024]{1,0:T(8,128)(2,1)S(1)} %get-tuple-element.20), channel_id=1, source_target_pairs={{0,2},{1,3},{2,0},{3,1},{4,6},{5,7},{6,4},{7,5},{8,10},{9,11},{10,... | collective-permute-start | bytes 393224 | tf_op jit(solution)/shard_map/ppermute | solution.py:103
  31.0 11.0 %collective-permute-start.4 = (bf16[64,1024]{1,0:T(8,128)(2,1)S(1)}, bf16[64,1024]{1,0:T(8,128)(2,1)S(1)}, u32[]{:S(2)}, u32[]{:S(2)}) collective-permute-start(bf16[64,1024]{1,0:T(8,128)(2,1)S(1)} %get-tuple-element.21), channel_id=1, source_target_pairs={{0,4},{1,5},{2,6},{3,7},{4,0},{5,1},{6,2},{7,3},{8,12},{9,13},{10,... | collective-permute-start | bytes 393224 | tf_op jit(solution)/shard_map/ppermute | solution.py:103
  33.0 13.5 %collective-permute-start.5 = (bf16[64,1024]{1,0:T(8,128)(2,1)S(1)}, bf16[64,1024]{1,0:T(8,128)(2,1)S(1)}, u32[]{:S(2)}, u32[]{:S(2)}) collective-permute-start(bf16[64,1024]{1,0:T(8,128)(2,1)S(1)} %get-tuple-element.22), channel_id=1, source_target_pairs={{0,6},{1,7},{2,4},{3,5},{4,2},{5,3},{6,0},{7,1},{8,14},{9,15},{10,... | collective-permute-start | bytes 393224 | tf_op jit(solution)/shard_map/ppermute | solution.py:103
